TPU v7x, 512 devices: a whole 4x8x8 slice. The times are simulated.
512 devices in a mesh: row: 16 (over x_hi, z), col: 32 (over y, x_lo, core).
Axes of the slice: x: 4 (x_hi: 2, x_lo: 2; x = x_hi * 2 + x_lo), y: 8, z: 8, core: 2. Of those that a mesh axis runs over, the one named last changes fastest.
Arguments:
- emb: float32 [32768, 128], P(('row', 'col')), may hold values from -1.8 to 1.8
- bias: float32 [32768], P(('row', 'col')), may hold values from -4 to 4
- emb_sq: float32 [32768, 128], P(('row', 'col')), may hold values from 10 to 1000
- bias_sq: float32 [32768], P(('row', 'col')), may hold values from 30000 to 3000000
- tile_rows: int32 [2048], P(('row', 'col')), may hold values from 0 to 15
- tile_cols: int32 [2048], P(('row', 'col')), may hold values from 0 to 7
- tile_live: int32 [512], P(('row', 'col')), may hold values from 1 to 4, 1024 in all
- counts: int32 [2048, 128, 128], P(('row', 'col')), may hold values from 0 to 1023
Outputs:
- emb_out: float32 [32768, 128], P(('row', 'col'))
- bias_out: float32 [32768], P(('row', 'col'))
Inputs may be any that keep to these rules, and one draw needn't show every extreme that they name: Each device uses its first tile_live slots and ignores the others; some device uses all 4.
All inputs are finite; a program needn't handle non-finite values.
Results may differ from a plain program's by a relative error of at most 0.005.
Values may be sent and summed in bfloat16 or wider, within the bound.
A program may use at most 64 MiB of HBM per device.

v0:
```python
import jax
import jax.numpy as jnp
from jax import lax
from jax.sharding import PartitionSpec as P

D = 128
TILE = 128
STEPS = 2


learn_rate = 0.1
count_cap = 100.0


def pair_weights(counts):
    amounts = counts.astype(jnp.float32)
    weight = jnp.minimum(1.0, jnp.power(amounts / count_cap, 0.75))
    target = jnp.log(jnp.maximum(amounts, 1.0))
    return (weight, target)


def tile_terms(
    rows_half, rows_bias, cols_half, cols_bias, rows_index, cols_index, live_count, weight, target
):
    row_tiles = rows_half.shape[0] // TILE
    col_tiles = cols_half.shape[0] // TILE
    left_tiles = rows_half.reshape(row_tiles, TILE, D)[rows_index]
    right_tiles = cols_half.reshape(col_tiles, TILE, D)[cols_index]
    left_bias = rows_bias.reshape(row_tiles, TILE)[rows_index].astype(jnp.float32)
    right_bias = cols_bias.reshape(col_tiles, TILE)[cols_index].astype(jnp.float32)
    scores = jnp.einsum("spd,sqd->spq", left_tiles, right_tiles, preferred_element_type=jnp.float32)
    errors = scores + left_bias[:, :, None] + right_bias[:, None, :] - target
    live_mask = jnp.arange(rows_index.shape[0]) < live_count
    residual = jnp.where(live_mask[:, None, None], weight * errors, 0.0)
    resid_half = residual.astype(jnp.bfloat16)
    grad_left = jnp.einsum(
        "spq,sqd->spd", resid_half, right_tiles, preferred_element_type=jnp.float32
    )
    grad_right = jnp.einsum(
        "spq,spd->sqd", resid_half, left_tiles, preferred_element_type=jnp.float32
    )
    row_onehot = (rows_index[:, None] == jnp.arange(row_tiles)[None, :]).astype(jnp.float32)
    col_onehot = (cols_index[:, None] == jnp.arange(col_tiles)[None, :]).astype(jnp.float32)
    highest = lax.Precision.HIGHEST
    row_part = jnp.einsum("sr,spd->rpd", row_onehot, grad_left, precision=highest).reshape(
        row_tiles * TILE, D
    )
    row_bpart = jnp.einsum(
        "sr,sp->rp", row_onehot, jnp.sum(residual, axis=2), precision=highest
    ).reshape(row_tiles * TILE)
    col_part = jnp.einsum("sr,sqd->rqd", col_onehot, grad_right, precision=highest).reshape(
        col_tiles * TILE, D
    )
    col_bpart = jnp.einsum(
        "sr,sq->rq", col_onehot, jnp.sum(residual, axis=1), precision=highest
    ).reshape(col_tiles * TILE)
    return (row_part, row_bpart, col_part, col_bpart)


def adagrad_step(values, accum, grads):
    new_accum = accum + grads * grads
    return (values - learn_rate * grads / jnp.sqrt(new_accum), new_accum)


def gather_columns(own_half, own_bias):
    return (
        lax.all_gather(own_half, "row", axis=0, tiled=True),
        lax.all_gather(own_bias, "row", axis=0, tiled=True),
    )


def return_rows(row_part, row_bpart):
    return (
        lax.psum_scatter(
            row_part.astype(jnp.bfloat16), "col", scatter_dimension=0, tiled=True
        ).astype(jnp.float32),
        lax.psum_scatter(
            row_bpart.astype(jnp.bfloat16), "col", scatter_dimension=0, tiled=True
        ).astype(jnp.float32),
    )


def return_columns(col_part, col_bpart):
    return (
        lax.psum_scatter(
            col_part.astype(jnp.bfloat16), "row", scatter_dimension=0, tiled=True
        ).astype(jnp.float32),
        lax.psum_scatter(
            col_bpart.astype(jnp.bfloat16), "row", scatter_dimension=0, tiled=True
        ).astype(jnp.float32),
    )


def per_device(emb, bias, emb_sq, bias_sq, tile_rows, tile_cols, tile_live, counts):
    weight, target = pair_weights(counts)
    live_count = tile_live[0]
    emb_now, bias_now, emb_accum, bias_accum = (emb, bias, emb_sq, bias_sq)
    for step_index in range(STEPS):
        emb_half = emb_now.astype(jnp.bfloat16)
        bias_half = bias_now.astype(jnp.bfloat16)
        rows_half, rows_bias = (
            lax.all_gather(emb_half, "col", axis=0, tiled=True),
            lax.all_gather(bias_half, "col", axis=0, tiled=True),
        )
        cols_half, cols_bias = gather_columns(emb_half, bias_half)
        row_part, row_bpart, col_part, col_bpart = tile_terms(
            rows_half,
            rows_bias,
            cols_half,
            cols_bias,
            tile_rows,
            tile_cols,
            live_count,
            weight,
            target,
        )
        own_rows, own_rbias = return_rows(row_part, row_bpart)
        own_cols, own_cbias = return_columns(col_part, col_bpart)
        emb_now, emb_accum = adagrad_step(emb_now, emb_accum, own_rows + own_cols)
        bias_now, bias_accum = adagrad_step(bias_now, bias_accum, own_rbias + own_cbias)
    return (emb_now, bias_now)


def solution(mesh):
    placed = (
        P(("row", "col"), None),
        P(("row", "col")),
        P(("row", "col"), None),
        P(("row", "col")),
        P(("row", "col")),
        P(("row", "col")),
        P(("row", "col")),
        P(("row", "col"), None, None),
    )
    return jax.shard_map(
        per_device,
        mesh=mesh,
        in_specs=placed,
        out_specs=(P(("row", "col"), None), P(("row", "col"))),
        check_vma=False,
    )
```

profile of v0, /device:TPU:1, one launch (start us, length us, event | category | flops | bytes accessed | tf_op | source)
XLA Modules:
  0.0 905.0 jit_solution(3973090360989484684)
XLA Ops:
  7.2 0.0 reduce-scatter.7.cloned.1.call-start
  7.2 0.8 convert_element_type.126
  8.0 42.0 %all_gather.25 = bf16[1024,128]{1,0:T(8,128)(2,1)S(1)} all-gather(bf16[64,128]{1,0:T(8,128)(2,1)S(1)} %convert_element_type.126), channel_id=1, replica_groups=mesh['row'=16,'col'=32] {'row'}, dimensions={0}, use_global_device_ids=true | all-gather | bytes 278528 | tf_op jit(solution)/shard_map/all_gather | solution.py:67
  50.0 43.0 %all_gather.24 = bf16[2048,128]{1,0:T(8,128)(2,1)S(1)} all-gather(bf16[64,128]{1,0:T(8,128)(2,1)S(1)} %convert_element_type.126), channel_id=1, replica_groups=mesh['row'=16,'col'=32] {'col'}, dimensions={0}, use_global_device_ids=true | all-gather | bytes 540672 | tf_op jit(solution)/shard_map/all_gather | solution.py:102
  93.6 0.6 copy-done.9
  94.3 0.6 copy-done.6
  94.9 0.6 copy-done.4
  95.6 0.7 copy-done.8
  96.3 0.7 fusion.44
  98.3 0.2 dynamic-update-slice.1
  98.5 29.7 %all-reduce.1 = bf16[1024]{0:T(1024)(128)(2,1)S(1)} all-reduce(bf16[1024]{0:T(1024)(128)(2,1)S(1)} %dynamic-update-slice.1), channel_id=1, replica_groups=mesh['row'=16,'col'=32] {'row'}, use_global_device_ids=true, to_apply=%add.1 | all-reduce | flops 1024 | bytes 4096
  128.3 0.6 gather_fusion.3
  128.9 0.2 dynamic-update-slice
  129.1 59.8 %all-reduce = bf16[2048]{0:T(1024)(128)(2,1)S(1)} all-reduce(bf16[2048]{0:T(1024)(128)(2,1)S(1)} %dynamic-update-slice), channel_id=1, replica_groups=mesh['row'=16,'col'=32] {'col'}, use_global_device_ids=true, to_apply=%add | all-reduce | flops 2048 | bytes 8192
  188.9 0.6 gather_fusion.2
  189.5 0.6 gather_fusion.1
  190.1 0.6 gather_fusion
  190.7 0.4 fusion.42
  191.1 0.2 fusion.20
  191.4 0.6 convolution_convert_fusion.3
  192.0 0.7 copy.18
  192.7 0.0 reduce-scatter.7.cloned.1.call-update
  192.7 0.0 reduce-scatter.5.cloned.1.call-start
  192.8 0.2 fusion.22
  193.0 0.8 convolution_convert_fusion.1
  193.8 0.9 copy.15
  194.7 0.0 reduce-scatter.5.cloned.1.call-update
  194.7 0.0 reduce-scatter.11.cloned.1.call-start
  196.1 0.3 fusion.10
  196.3 31.1 %all-reduce.5 = bf16[1024]{0:T(1024)(128)(2,1)S(1)} all-reduce(bf16[1024]{0:T(1024)(128)(2,1)S(1)} %fusion.10), channel_id=5, replica_groups=mesh['row'=16,'col'=32] {'row'}, use_global_device_ids=true, to_apply=%region_5.6.clone | all-reduce | flops 1024 | bytes 4096
  227.4 0.3 fusion.8
  227.7 60.3 %all-reduce.4 = bf16[2048]{0:T(1024)(128)(2,1)S(1)} all-reduce(bf16[2048]{0:T(1024)(128)(2,1)S(1)} %fusion.8), channel_id=4, replica_groups=mesh['row'=16,'col'=32] {'col'}, use_global_device_ids=true, to_apply=%region_3.4.clone | all-reduce | flops 2048 | bytes 8192
  288.0 0.1 fusion.43
  288.1 0.2 dynamic-update-slice.3
  288.3 0.2 dynamic-update-slice.2
  288.5 53.0 %all-reduce.2 = bf16[2048]{0:T(1024)(128)(2,1)S(1)} all-reduce(bf16[2048]{0:T(1024)(128)(2,1)S(1)} %dynamic-update-slice.2), channel_id=1, replica_groups=mesh['row'=16,'col'=32] {'col'}, use_global_device_ids=true, to_apply=%add.2 | all-reduce | flops 2048 | bytes 8192
  341.6 0.6 gather_fusion.6
  342.1 30.5 %all-reduce.3 = bf16[1024]{0:T(1024)(128)(2,1)S(1)} all-reduce(bf16[1024]{0:T(1024)(128)(2,1)S(1)} %dynamic-update-slice.3), channel_id=1, replica_groups=mesh['row'=16,'col'=32] {'row'}, use_global_device_ids=true, to_apply=%add.3 | all-reduce | flops 1024 | bytes 4096
  372.7 0.6 gather_fusion.7
  373.2 10.8 %reduce-scatter.7.cloned.1.call-done = bf16[64,128]{1,0:T(8,128)(2,1)} async-done(((bf16[1024,128]{1,0:T(8,128)(2,1)}), bf16[64,128]{1,0:T(8,128)(2,1)}) %reduce-scatter.7.cloned.1.call-update) | async-done | bytes 16400 | tf_op jit(solution)/shard_map/reduce_scatter | solution.py:85
  384.0 120.7 %reduce-scatter.5.cloned.1.call-done = bf16[64,128]{1,0:T(8,128)(2,1)} async-done(((bf16[2048,128]{1,0:T(8,128)(2,1)}), bf16[64,128]{1,0:T(8,128)(2,1)}) %reduce-scatter.5.cloned.1.call-update) | async-done | bytes 16400 | tf_op jit(solution)/shard_map/reduce_scatter | solution.py:74
  504.7 0.8 fusion.24
  505.5 35.3 %all_gather.29 = bf16[1024,128]{1,0:T(8,128)(2,1)S(1)} all-gather(bf16[64,128]{1,0:T(8,128)(2,1)S(1)} %fusion.24), channel_id=1, replica_groups=mesh['row'=16,'col'=32] {'row'}, dimensions={0}, use_global_device_ids=true | all-gather | bytes 278528 | tf_op jit(solution)/shard_map/all_gather | solution.py:67
  540.8 42.4 %all_gather.28 = bf16[2048,128]{1,0:T(8,128)(2,1)S(1)} all-gather(bf16[64,128]{1,0:T(8,128)(2,1)S(1)} %fusion.24), channel_id=1, replica_groups=mesh['row'=16,'col'=32] {'col'}, dimensions={0}, use_global_device_ids=true | all-gather | bytes 540672 | tf_op jit(solution)/shard_map/all_gather | solution.py:102
  583.2 0.6 gather_fusion.5
  583.8 0.6 gather_fusion.4
  584.4 0.4 fusion.41
  584.8 0.2 fusion.16
  585.1 0.6 convolution_convert_fusion.2
  585.7 0.7 copy.23
  586.4 0.0 reduce-scatter.11.cloned.1.call-update
  586.5 0.0 reduce-scatter.9.cloned.1.call-start
  586.5 0.2 fusion.18
  586.7 0.8 convolution_convert_fusion
  587.5 0.9 copy.20
  588.4 0.0 reduce-scatter.9.cloned.1.call-update
  588.4 0.3 fusion.11
  588.7 29.7 %all-reduce.7 = bf16[1024]{0:T(1024)(128)(2,1)S(1)} all-reduce(bf16[1024]{0:T(1024)(128)(2,1)S(1)} %fusion.11), channel_id=9, replica_groups=mesh['row'=16,'col'=32] {'row'}, use_global_device_ids=true, to_apply=%region_11.12.clone | all-reduce | flops 1024 | bytes 4096
  618.4 0.3 fusion.9
  618.7 59.5 %all-reduce.6 = bf16[2048]{0:T(1024)(128)(2,1)S(1)} all-reduce(bf16[2048]{0:T(1024)(128)(2,1)S(1)} %fusion.9), channel_id=8, replica_groups=mesh['row'=16,'col'=32] {'col'}, use_global_device_ids=true, to_apply=%region_9.10.clone | all-reduce | flops 2048 | bytes 8192
  678.2 0.6 multiply_subtract_fusion.2
  678.8 97.3 %reduce-scatter.11.cloned.1.call-done = bf16[64,128]{1,0:T(8,128)(2,1)} async-done(((bf16[1024,128]{1,0:T(8,128)(2,1)}), bf16[64,128]{1,0:T(8,128)(2,1)}) %reduce-scatter.11.cloned.1.call-update) | async-done | bytes 16400 | tf_op jit(solution)/shard_map/reduce_scatter | solution.py:85
  776.1 121.0 %reduce-scatter.9.cloned.1.call-done = bf16[64,128]{1,0:T(8,128)(2,1)} async-done(((bf16[2048,128]{1,0:T(8,128)(2,1)}), bf16[64,128]{1,0:T(8,128)(2,1)}) %reduce-scatter.9.cloned.1.call-update) | async-done | bytes 16400 | tf_op jit(solution)/shard_map/reduce_scatter | solution.py:74
  897.1 1.4 multiply_subtract_fusion
  (32 shorter events, 0.1 us)
Async XLA Ops:
  7.2 376.9 %reduce-scatter.7.cloned.1.call-start = ((), (), s32[]{:S(2)}) async-start(), calls=%async_computation.5 | async-start | bytes 278528 | tf_op jit(solution)/shard_map/reduce_scatter | solution.py:85
  93.6 0.7 copy-start.9
  94.3 0.7 copy-start.6
  94.9 0.7 copy-start.4
  95.6 0.7 copy-start.8
  95.6 0.7 copy-start.7
  189.5 1.2 copy-start.10
  192.7 312.0 %reduce-scatter.5.cloned.1.call-start = ((), (), s32[]{:S(2)}) async-start(), calls=%async_computation.4 | async-start | bytes 540672 | tf_op jit(solution)/shard_map/reduce_scatter | solution.py:74
  194.7 581.3 %reduce-scatter.11.cloned.1.call-start = ((), (), s32[]{:S(2)}) async-start(), calls=%async_computation.7 | async-start | bytes 278528 | tf_op jit(solution)/shard_map/reduce_scatter | solution.py:85
  196.1 91.9 %copy-start.5 = (f32[64]{0:T(128)S(1)}, f32[64]{0:T(128)}, u32[]{:S(2)}) copy-start(f32[64]{0:T(128)} %param.11) | copy-start | bytes 772
  227.7 277.0 %copy-start = (f32[64,128]{1,0:T(8,128)S(1)}, f32[64,128]{1,0:T(8,128)}, u32[]{:S(2)}) copy-start(f32[64,128]{1,0:T(8,128)} %param.8) | copy-start | bytes 98308
  227.7 277.0 %copy-start.1 = (f32[64,128]{1,0:T(8,128)S(1)}, f32[64,128]{1,0:T(8,128)}, u32[]{:S(2)}) copy-start(f32[64,128]{1,0:T(8,128)} %param.10) | copy-start | bytes 98308
  586.5 310.6 %reduce-scatter.9.cloned.1.call-start = ((), (), s32[]{:S(2)}) async-start(), calls=%async_computation.6 | async-start | bytes 540672 | tf_op jit(solution)/shard_map/reduce_scatter | solution.py:74
  618.4 278.7 %copy-start.2 = (bf16[64,128]{1,0:T(8,128)(2,1)S(1)}, bf16[64,128]{1,0:T(8,128)(2,1)}, u32[]{:S(2)}) copy-start(bf16[64,128]{1,0:T(8,128)(2,1)} %reduce-scatter.7.cloned.1.call-done) | copy-start | bytes 49156
  618.4 278.7 %copy-start.3 = (bf16[64,128]{1,0:T(8,128)(2,1)S(1)}, bf16[64,128]{1,0:T(8,128)(2,1)}, u32[]{:S(2)}) copy-start(bf16[64,128]{1,0:T(8,128)(2,1)} %reduce-scatter.5.cloned.1.call-done) | copy-start | bytes 49156
Sparse Core Ops, SparseCore 0:
  192.9 191.1 reduce-scatter.6
  387.0 117.6 reduce-scatter.4
  586.6 189.4 reduce-scatter.10
  778.9 118.1 reduce-scatter.8
where the time goes:
time: 907 us; the launch traced here: 905 us
  blocking collectives  516 us (57%)
  waiting for transfers between devices  350 us (39%)
  between operations  17.3 us (2%)
  local copies, waits for them, and re-layouts  12.1 us (1%)
    unnamed x8, blocking collectives  354 us
    reduce_scatter x2, waiting for transfers between devices, return_rows(): lax.psum_scatter(row_part.astype(jnp.bfloat16), 'col', scatter_dimension=...  242 us
    reduce_scatter x2, waiting for transfers between devices, return_columns(): lax.psum_scatter(col_part.astype(jnp.bfloat16), 'row', scatter_dimension=...  108 us
    all_gather x2, blocking collectives, per_device(): lax.all_gather(emb_half, 'col', axis=0, tiled=True)  85.4 us
    all_gather x2, blocking collectives, gather_columns(): lax.all_gather(own_half, 'row', axis=0, tiled=True)  77.3 us
  transfers between devices with their start and end apart: 4, of which 4 were waited for; matrix products, arithmetic and copies ran while one was open for 1% of the time, Pallas kernels for 0%

commit v1 on v0

v1 whole, which is shorter than its diff:
```python
import functools

import jax
import jax.numpy as jnp
from jax import lax
from jax.experimental import pallas as pl
from jax.experimental.pallas import tpu as pltpu
from jax.sharding import PartitionSpec as P

MESH = pl.DeviceIdType.MESH
D = 128
TILE = 128
HALF = 64
NT = 4
STEPS = 2
RW = 80
ROW_TILES = 16
COL_TILES = 8
NEAR = 15

learn_rate = 0.1
count_cap = 100.0

F32 = jnp.float32
BF16 = jnp.bfloat16


ROW_OFF = sorted(
    [(a, b) for a in range(8) for b in range(2) if a or b], key=lambda o: -(min(o[0], 8 - o[0]) + o[1])
)
COL_OFF = sorted(
    [(a, b) for a in range(8) for b in range(2) if a or b], key=lambda o: -(min(o[0], 8 - o[0]) + 2 * o[1])
)


def dot(a, b, dims):
    return lax.dot_general(a, b, (dims, ((), ())), preferred_element_type=F32)


def body(
    emb_hbm, bias_hbm, esq_hbm, bsq_hbm, counts_hbm, trow, tcol, tlive,
    emb_out, bias_out,
    vals, bvals, acc, bacc, cnt, weight, target,
    msg, rowbuf, colbuf, gleft, gright, gbias, xsend, xrecv, rsend, rrecv, csend, crecv,
    in_sem, ag_ss, ag_rs, fw_ss, fw_rs, rs_ss, rs_rs,
):
    r, c = lax.axis_index("row"), lax.axis_index("col")
    xh, z = r // 8, r % 8
    y, xl, co = c // 4, (c // 2) % 2, c % 2
    chip = c // 2

    def row_chip(off):
        return ((y + off[0]) % 8) * 2 + (xl + off[1]) % 2

    def col_rank(off):
        return ((xh + off[1]) % 2) * 8 + (z + off[0]) % 8

    def row_src(off):
        return ((y + 8 - off[0]) % 8) * 2 + (xl + 2 - off[1]) % 2

    def col_src(off):
        return ((xh + 2 - off[1]) % 2) * 8 + (z + 8 - off[0]) % 8

    other = (r, chip * 2 + 1 - co)

    loads = [
        pltpu.make_async_copy(emb_hbm, vals, in_sem.at[0]),
        pltpu.make_async_copy(esq_hbm, acc, in_sem.at[1]),
        pltpu.make_async_copy(counts_hbm, cnt, in_sem.at[2]),
        pltpu.make_async_copy(bias_hbm, bvals, in_sem.at[3]),
        pltpu.make_async_copy(bsq_hbm, bacc, in_sem.at[4]),
    ]
    for load in loads:
        load.start()

    barrier = pltpu.get_barrier_semaphore()
    for off in ROW_OFF:
        pl.semaphore_signal(barrier, inc=1, device_id=(r, row_chip(off) * 2 + co), device_id_type=MESH)
    for off in COL_OFF:
        pl.semaphore_signal(barrier, inc=1, device_id=(col_rank(off), c), device_id_type=MESH)
    pl.semaphore_signal(barrier, inc=1, device_id=other, device_id_type=MESH)

    loads[0].wait()
    loads[1].wait()
    loads[3].wait()
    loads[4].wait()
    live = tlive[0]
    gleft[NT] = jnp.zeros((2, HALF, D), BF16)
    gright[NT] = jnp.zeros((2, HALF, D), BF16)
    gbias[NT] = jnp.zeros((2, 16, D), BF16)
    low_lanes = lax.broadcasted_iota(jnp.int32, (16, D), 1) < HALF
    first_row = lax.broadcasted_iota(jnp.int32, (16, D), 0)
    one_rows = jnp.ones((16, D), BF16)

    pl.semaphore_wait(barrier, 2 * NEAR + 1)

    for step in range(STEPS):
        sends = []
        msg[step, 0:HALF] = vals[...].astype(BF16)
        msg[step, HALF:RW] = jnp.broadcast_to(bvals[...], (RW - HALF, D)).astype(BF16)
        row_copies, col_copies = [], []
        for k, off in enumerate(ROW_OFF):
            row_copies.append(
                pltpu.make_async_remote_copy(
                    src_ref=msg.at[step], dst_ref=rowbuf.at[step, c],
                    send_sem=ag_ss.at[step, k], recv_sem=ag_rs.at[step, k],
                    device_id=(r, row_chip(off) * 2 + co), device_id_type=MESH,
                )
            )
        for k, off in enumerate(COL_OFF):
            col_copies.append(
                pltpu.make_async_remote_copy(
                    src_ref=msg.at[step], dst_ref=colbuf.at[step, r],
                    send_sem=ag_ss.at[step, NEAR + k], recv_sem=ag_rs.at[step, NEAR + k],
                    device_id=(col_rank(off), c), device_id_type=MESH,
                )
            )
        for a, b in zip(row_copies, col_copies):
            a.start()
            b.start()
        own = pltpu.make_async_remote_copy(
            src_ref=msg.at[step], dst_ref=rowbuf.at[step, c],
            send_sem=fw_ss.at[step, NEAR], recv_sem=fw_rs.at[step, NEAR],
            device_id=other, device_id_type=MESH,
        )
        own.start()
        sends += row_copies + col_copies + [own]
        rowbuf[step, c] = msg[step]
        colbuf[step, r] = msg[step]

        if step == 0:
            loads[2].wait()
            for s in range(NT):
                amounts = cnt[s].astype(F32)
                share = amounts / count_cap
                root = jnp.sqrt(share)
                w = jnp.minimum(1.0, root * jnp.sqrt(root))
                weight[s] = jnp.where(s < live, w, 0.0)
                target[s] = jnp.log(jnp.maximum(amounts, 1.0))

        forwards = []
        for k in reversed(range(NEAR)):
            row_copies[k].wait_recv()
            slot = row_src(ROW_OFF[k]) * 2 + co
            forward = pltpu.make_async_remote_copy(
                src_ref=rowbuf.at[step, slot], dst_ref=rowbuf.at[step, slot],
                send_sem=fw_ss.at[step, k], recv_sem=fw_rs.at[step, k],
                device_id=other, device_id_type=MESH,
            )
            forward.start()
            forwards.append(forward)
        sends += forwards
        for copy in col_copies:
            copy.wait_recv()
        own.wait_recv()
        for forward in forwards:
            forward.wait_recv()

        lefts, rights = [], []
        for s in range(NT):
            ti, tj = trow[s], tcol[s]
            e_i = rowbuf[step, pl.ds(2 * ti, 2), 0:HALF, :].reshape(TILE, D)
            e_j = colbuf[step, pl.ds(2 * tj, 2), 0:HALF, :].reshape(TILE, D)
            b_i = jnp.where(low_lanes, rowbuf[step, 2 * ti, HALF:RW, :], rowbuf[step, 2 * ti + 1, HALF:RW, :])
            b_j = jnp.where(low_lanes, colbuf[step, 2 * tj, HALF:RW, :], colbuf[step, 2 * tj + 1, HALF:RW, :])
            zero = jnp.zeros((16, D), BF16)
            one = jnp.ones((16, D), BF16)
            lhs = jnp.where(first_row == 0, b_i, jnp.where(first_row == 1, one, zero))
            rhs = jnp.where(first_row == 0, one, jnp.where(first_row == 1, b_j, zero))
            score = dot(e_i, e_j, ((1,), (1,))) + dot(lhs, rhs, ((0,), (0,)))
            resid = (weight[s] * (score - target[s])).astype(BF16)
            lefts.append((dot(resid, e_j, ((1,), (0,))), dot(one_rows, resid, ((1,), (1,)))))
            rights.append((dot(resid, e_i, ((0,), (0,))), dot(one_rows, resid, ((1,), (0,)))))

        for store, side, terms, ids in ((gleft, 0, lefts, trow), (gright, 1, rights, tcol)):
            for s in range(NT):
                total, btotal = terms[s]
                for o in range(NT):
                    if o != s:
                        same = jnp.where(ids[o] == ids[s], 1.0, 0.0)
                        total = total + same * terms[o][0]
                        btotal = btotal + same * terms[o][1]
                store[s] = total.astype(BF16).reshape(2, HALF, D)
                gbias[s, side] = btotal.astype(BF16)

        def slot_of(ids, tile):
            found = jnp.int32(NT)
            for s in range(NT):
                found = jnp.where(ids[s] == tile, s, found)
            return found

        row_slots = [slot_of(trow, t) for t in range(ROW_TILES)]
        for t in range(ROW_TILES):
            xsend[step, t, 0:HALF] = gleft[row_slots[t], 1 - co]
            xsend[step, t, HALF:RW] = gbias[row_slots[t], 0]
        cross = pltpu.make_async_remote_copy(
            src_ref=xsend.at[step], dst_ref=xrecv.at[step],
            send_sem=rs_ss.at[step, 2 * NEAR], recv_sem=rs_rs.at[step, 2 * NEAR],
            device_id=other, device_id_type=MESH,
        )
        cross.start()
        sends.append(cross)
        for t in range(COL_TILES):
            slot = slot_of(tcol, t)
            for h in range(2):
                csend[step, 2 * t + h, 0:HALF] = gright[slot, h]
                csend[step, 2 * t + h, HALF:RW] = gbias[slot, 1]
        col_copies = []
        for k, off in enumerate(COL_OFF):
            copy = pltpu.make_async_remote_copy(
                src_ref=csend.at[step, col_rank(off)], dst_ref=crecv.at[step, k],
                send_sem=rs_ss.at[step, NEAR + k], recv_sem=rs_rs.at[step, NEAR + k],
                device_id=(col_rank(off), c), device_id_type=MESH,
            )
            copy.start()
            col_copies.append(copy)
        sends += col_copies
        cross.wait_recv()
        for t in range(ROW_TILES):
            rsend[step, t, 0:HALF] = (
                gleft[row_slots[t], co].astype(F32) + xrecv[step, t, 0:HALF].astype(F32)
            ).astype(BF16)
            rsend[step, t, HALF:RW] = (
                gbias[row_slots[t], 0].astype(F32) + xrecv[step, t, HALF:RW].astype(F32)
            ).astype(BF16)
        row_copies = []
        for k, off in enumerate(ROW_OFF):
            copy = pltpu.make_async_remote_copy(
                src_ref=rsend.at[step, row_chip(off)], dst_ref=rrecv.at[step, k],
                send_sem=rs_ss.at[step, k], recv_sem=rs_rs.at[step, k],
                device_id=(r, row_chip(off) * 2 + co), device_id_type=MESH,
            )
            copy.start()
            row_copies.append(copy)
        sends += row_copies

        grad = rsend[step, chip].astype(F32)
        cgrad = csend[step, r].astype(F32)
        for k in reversed(range(NEAR)):
            col_copies[k].wait_recv()
            cgrad = cgrad + crecv[step, k].astype(F32)
        for k in reversed(range(NEAR)):
            row_copies[k].wait_recv()
            grad = grad + rrecv[step, k].astype(F32)

        g = grad[0:HALF] + cgrad[0:HALF]
        new_acc = acc[...] + g * g
        new_vals = vals[...] - learn_rate * g / jnp.sqrt(new_acc)
        lane_half = lax.broadcasted_iota(jnp.int32, (8, D), 1) // HALF
        row_b = jnp.where(lane_half == co, grad[HALF:HALF + 8], 0.0)
        col_b = jnp.where(lane_half == z % 2, cgrad[HALF:HALF + 8], 0.0)
        bg = row_b + pltpu.roll(row_b, HALF, 1) + col_b + pltpu.roll(col_b, HALF, 1)
        bg = bg[0:1]
        new_bacc = bacc[...] + bg * bg
        new_bvals = bvals[...] - learn_rate * bg / jnp.sqrt(new_bacc)
        if step + 1 < STEPS:
            vals[...] = new_vals
            acc[...] = new_acc
            bvals[...] = new_bvals
            bacc[...] = new_bacc
        else:
            emb_out[...] = new_vals
            bias_out[...] = new_bvals
        for copy in sends:
            copy.wait_send()


def per_device(emb, bias, emb_sq, bias_sq, tile_rows, tile_cols, tile_live, counts):
    twice = lambda v: jnp.concatenate([v, v]).reshape(1, D)
    any_spec = pl.BlockSpec(memory_space=pl.ANY)
    smem = pl.BlockSpec(memory_space=pltpu.SMEM)
    vmem = pl.BlockSpec(memory_space=pltpu.VMEM)
    emb_out, bias_out = pl.pallas_call(
        body,
        out_shape=(jax.ShapeDtypeStruct((HALF, D), F32), jax.ShapeDtypeStruct((1, D), F32)),
        in_specs=[any_spec] * 5 + [smem] * 3,
        out_specs=(vmem, vmem),
        scratch_shapes=[
            pltpu.VMEM((HALF, D), F32),
            pltpu.VMEM((1, D), F32),
            pltpu.VMEM((HALF, D), F32),
            pltpu.VMEM((1, D), F32),
            pltpu.VMEM((NT, TILE, TILE), jnp.int32),
            pltpu.VMEM((NT, TILE, TILE), F32),
            pltpu.VMEM((NT, TILE, TILE), F32),
            pltpu.VMEM((STEPS, RW, D), BF16),
            pltpu.VMEM((STEPS, 2 * ROW_TILES, RW, D), BF16),
            pltpu.VMEM((STEPS, 2 * COL_TILES, RW, D), BF16),
            pltpu.VMEM((NT + 1, 2, HALF, D), BF16),
            pltpu.VMEM((NT + 1, 2, HALF, D), BF16),
            pltpu.VMEM((NT + 1, 2, 16, D), BF16),
            pltpu.VMEM((STEPS, ROW_TILES, RW, D), BF16),
            pltpu.VMEM((STEPS, ROW_TILES, RW, D), BF16),
            pltpu.VMEM((STEPS, ROW_TILES, RW, D), BF16),
            pltpu.VMEM((STEPS, NEAR, RW, D), BF16),
            pltpu.VMEM((STEPS, 2 * COL_TILES, RW, D), BF16),
            pltpu.VMEM((STEPS, NEAR, RW, D), BF16),
            pltpu.SemaphoreType.DMA((5,)),
            pltpu.SemaphoreType.DMA((STEPS, 2 * NEAR)),
            pltpu.SemaphoreType.DMA((STEPS, 2 * NEAR)),
            pltpu.SemaphoreType.DMA((STEPS, NEAR + 1)),
            pltpu.SemaphoreType.DMA((STEPS, NEAR + 1)),
            pltpu.SemaphoreType.DMA((STEPS, 2 * NEAR + 1)),
            pltpu.SemaphoreType.DMA((STEPS, 2 * NEAR + 1)),
        ],
        compiler_params=pltpu.CompilerParams(
            collective_id=0, has_side_effects=True, vmem_limit_bytes=40 * 1024 * 1024
        ),
    )(emb, twice(bias), emb_sq, twice(bias_sq), counts, tile_rows, tile_cols, tile_live)
    return (emb_out, bias_out[0, :HALF])


def solution(mesh):
    placed = (
        P(("row", "col"), None),
        P(("row", "col")),
        P(("row", "col"), None),
        P(("row", "col")),
        P(("row", "col")),
        P(("row", "col")),
        P(("row", "col")),
        P(("row", "col"), None, None),
    )
    return jax.shard_map(
        per_device,
        mesh=mesh,
        in_specs=placed,
        out_specs=(P(("row", "col"), None), P(("row", "col"))),
        check_vma=False,
    )
```

time: 907 us -> 70.2 us (0.08)
  blocking collectives: 516 us -> 0 us
  waiting for transfers between devices: 350 us -> 0 us
  Pallas kernels: 0 us -> 64.2 us
  between operations: 17.3 us -> 1.34 us
    unnamed x8 -> x0, blocking collectives: 354 us -> none
    reduce_scatter x4 -> x0, waiting for transfers between devices: 350 us -> none  [the longest x2 242 us: return_rows(): lax.psum_scatter(row_part.astype(jnp.bfloat16), 'col', scatter_dimension=...]
    all_gather x4 -> x0, blocking collectives: 163 us -> none  [the longest x2 85.4 us: per_device(): lax.all_gather(emb_half, 'col', axis=0, tiled=True)]
    pallas_call x0 -> x1, Pallas kernels: none -> 64.2 us  [per_device(): pl.pallas_call(body, out_shape=(jax.ShapeDtypeStruct((HALF, D), F32), jax...]
  transfers between devices with their start and end apart: 4 -> 0, of which waited for: 4 -> 0; matrix products, arithmetic and copies ran while one was open for 1% -> 0% of each run, Pallas kernels for 0% -> 0%
where the time goes in v1:
time: 70.2 us; the launch traced here: 69.9 us
  Pallas kernels  64.2 us (91%)
  local copies, waits for them, and re-layouts  4.27 us (6%)
  between operations  1.34 us (2%)
    pallas_call x1, Pallas kernels, per_device(): pl.pallas_call(body, out_shape=(jax.ShapeDtypeStruct((HALF, D), F32), jax...  64.2 us
    unnamed x15, local copies, waits for them, and re-layouts  3.76 us

profile of v1, /device:TPU:1, one launch (start us, length us, event | category | flops | bytes accessed | tf_op | source)
XLA Modules:
  0.0 69.9 jit_solution(8666442570802249253)
XLA Ops:
  0.6 0.0 copy-start.6
  0.6 0.0 copy-start.5
  1.3 0.0 copy-done.6
  1.3 0.0 copy-done.5
  1.3 0.1 maximum_bitcast_fusion
  1.4 0.0 copy-start.3
  1.4 0.0 copy-start.4
  1.4 0.7 copy-done.3
  2.1 0.0 copy-done.4
  2.1 0.0 copy-start
  2.1 0.9 %copy-done = s32[4,128,128]{2,1,0:T(8,128)S(1)} copy-done((s32[4,128,128]{2,1,0:T(8,128)S(1)}, s32[4,128,128]{2,1,0:T(8,128)}, u32[]{:S(2)}) %copy-start) | copy-done | bytes 262168
  3.0 0.0 copy-start.1
  3.0 0.8 %copy-done.1 = f32[64,128]{1,0:T(8,128)S(1)} copy-done((f32[64,128]{1,0:T(8,128)S(1)}, f32[64,128]{1,0:T(8,128)}, u32[]{:S(2)}) %copy-start.1) | copy-done | bytes 32792
  3.8 0.0 copy-start.2
  3.8 0.8 %copy-done.2 = f32[64,128]{1,0:T(8,128)S(1)} copy-done((f32[64,128]{1,0:T(8,128)S(1)}, f32[64,128]{1,0:T(8,128)}, u32[]{:S(2)}) %copy-start.2) | copy-done | bytes 32792
  4.6 64.2 %shard_map.95 = (f32[64,128]{1,0:T(8,128)S(1)}, f32[1,128]{1,0:T(1,128)S(1)}) custom-call(f32[64,128]{1,0:T(8,128)S(1)} %copy-done.1, f32[1,128]{1,0:T(1,128)S(1)} %get-tuple-element.6.bias_hbm, f32[64,128]{1,0:T(8,128)S(1)} %copy-done.2, f32[1,128]{1,0:T(1,128)S(1)} %get-tuple-element.7.bsq_hbm, s32[4,128,128]{2,1,0:T(8,128)S(1)} %copy-done, ...), custom_call_target="tpu_custom_call" | custom-call | tf_op jit(solution)/shard_map/pallas_call | solution.py:273
  68.8 0.5 slice_bitcast_fusion
  69.3 0.6 copy.12
Async XLA Ops:
  0.6 0.7 copy-start.6
  0.6 0.7 copy-start.5
  1.4 0.7 copy-start.3
  1.4 0.7 copy-start.4
  2.1 0.9 %copy-start = (s32[4,128,128]{2,1,0:T(8,128)S(1)}, s32[4,128,128]{2,1,0:T(8,128)}, u32[]{:S(2)}) copy-start(s32[4,128,128]{2,1,0:T(8,128)} %counts_hbm.1) | copy-start | bytes 786436
  3.0 0.8 %copy-start.1 = (f32[64,128]{1,0:T(8,128)S(1)}, f32[64,128]{1,0:T(8,128)}, u32[]{:S(2)}) copy-start(f32[64,128]{1,0:T(8,128)} %emb_hbm.1) | copy-start | bytes 98308
  3.8 0.8 %copy-start.2 = (f32[64,128]{1,0:T(8,128)S(1)}, f32[64,128]{1,0:T(8,128)}, u32[]{:S(2)}) copy-start(f32[64,128]{1,0:T(8,128)} %esq_hbm.1) | copy-start | bytes 98308

commit v2 on v0

v2 whole, which is shorter than its diff:
```python
import jax
import jax.numpy as jnp
from jax import lax
from jax.experimental import pallas as pl
from jax.experimental.pallas import tpu as pltpu
from jax.sharding import PartitionSpec as P

MESH = pl.DeviceIdType.MESH
D = 128
TILE = 128
HALF = 64
NT = 4
STEPS = 2
ROW_TILES = 16
COL_TILES = 8
NEAR = 15
GROUPS = 3
PER = NEAR // GROUPS

learn_rate = 0.1
count_cap = 100.0

F32 = jnp.float32
BF16 = jnp.bfloat16

OFFSETS = [(a, b) for a in range(8) for b in range(2) if a or b]
ROW_OFF = sorted(OFFSETS, key=lambda o: -(min(o[0], 8 - o[0]) + o[1]))
COL_OFF = sorted(OFFSETS, key=lambda o: -(min(o[0], 8 - o[0]) + 2 * o[1]))


def dot(a, b, dims):
    return lax.dot_general(a, b, (dims, ((), ())), preferred_element_type=F32)


def body(
    emb_hbm, bias_hbm, esq_hbm, bsq_hbm, counts_hbm, trow_hbm, tcol_hbm, tlive_hbm,
    emb_out, bias_out,
    vals, bhalf, acc, bsqhalf, bvals, bacc, cnt, weight, target,
    trow, tcol, tlive, orow_in, orow,
    msg, bmsg, rowbuf, rowb, colbuf, colb, xsend, xbsend, xrecv, xbrecv,
    gown, goth, gbias, gright, cbias, hrecv, hbrecv,
    rsend, rbsend, rrecv, rbrecv, csend, cbsend, crecv, cbrecv,
    in_sem, id_ss, id_rs, ag_ss, ag_rs, x_ss, x_rs, rs_ss, rs_rs, rsb_ss, rsb_rs,
):
    r, c = lax.axis_index("row"), lax.axis_index("col")
    xh, z = r // 8, r % 8
    y, xl, co = c // 4, (c // 2) % 2, c % 2
    chip = c // 2

    def row_chip(off):
        return ((y + off[0]) % 8) * 2 + (xl + off[1]) % 2

    def col_rank(off):
        return ((xh + off[1]) % 2) * 8 + (z + off[0]) % 8

    other = (r, chip * 2 + 1 - co)

    def remote(src, dst, ss, rs, device):
        return pltpu.make_async_remote_copy(
            src_ref=src, dst_ref=dst, send_sem=ss, recv_sem=rs, device_id=device, device_id_type=MESH
        )

    def wait_bytes(ref, sem):
        pltpu.make_async_copy(ref, ref, sem).wait()

    loads = [
        pltpu.make_async_copy(src, dst, in_sem.at[i])
        for i, (src, dst) in enumerate(
            (
                (emb_hbm, vals), (bias_hbm, bhalf), (esq_hbm, acc), (bsq_hbm, bsqhalf),
                (counts_hbm, cnt), (trow_hbm, trow), (tcol_hbm, tcol), (tlive_hbm, tlive),
            )
        )
    ]
    for load in loads:
        load.start()

    barrier = pltpu.get_barrier_semaphore()
    for row_off, col_off in zip(ROW_OFF, COL_OFF):
        pl.semaphore_signal(barrier, inc=1, device_id=(col_rank(col_off), c), device_id_type=MESH)
        pl.semaphore_signal(barrier, inc=1, device_id=(r, row_chip(row_off) * 2 + co), device_id_type=MESH)
    pl.semaphore_signal(barrier, inc=1, device_id=other, device_id_type=MESH)

    for load in loads[:4] + loads[5:]:
        load.wait()
    live = tlive[0]
    for store in (gown, hrecv):
        store[NT] = jnp.zeros((HALF, D), BF16)
    gright[NT] = jnp.zeros((2, HALF, D), BF16)
    for store in (gbias, cbias, hbrecv):
        store[NT] = jnp.zeros((1, D), F32)
    bvals[...] = jnp.concatenate([bhalf[...], bhalf[...]], axis=1)
    bacc[...] = jnp.concatenate([bsqhalf[...], bsqhalf[...]], axis=1)
    low = lax.broadcasted_iota(jnp.int32, (1, D), 1) < HALF
    first_row = lax.broadcasted_iota(jnp.int32, (16, D), 0)
    one_rows = jnp.ones((16, D), BF16)

    pl.semaphore_wait(barrier, 2 * NEAR + 1)

    ids = remote(trow_hbm, orow_in, id_ss, id_rs, other)
    for step in range(STEPS):
        half = vals[...].astype(BF16)
        msg[step] = half
        bhalf_now = bvals[...].astype(BF16).astype(F32)
        bmsg[step] = bhalf_now
        for row_off, col_off in zip(ROW_OFF, COL_OFF):
            remote(bmsg.at[step], rowb.at[step, chip], ag_ss.at[step, 0], ag_rs.at[step, 0],
                   (r, row_chip(row_off) * 2 + co)).start()
            remote(bmsg.at[step], colb.at[step, r], ag_ss.at[step, 1], ag_rs.at[step, 1],
                   (col_rank(col_off), c)).start()
        for row_off, col_off in zip(ROW_OFF, COL_OFF):
            remote(msg.at[step], rowbuf.at[step, chip], ag_ss.at[step, 2], ag_rs.at[step, 2],
                   (r, row_chip(row_off) * 2 + co)).start()
            remote(msg.at[step], colbuf.at[step, r], ag_ss.at[step, 3], ag_rs.at[step, 3],
                   (col_rank(col_off), c)).start()
        rowbuf[step, chip] = half
        colbuf[step, r] = half
        rowb[step, chip] = bhalf_now
        colb[step, r] = bhalf_now

        if step == 0:
            ids.start()
            loads[4].wait()
            for s in range(NT):
                for h in range(2):
                    start = pl.multiple_of((co if h == 0 else 1 - co) * HALF, HALF)
                    amounts = cnt[s, pl.ds(start, HALF), :].astype(F32)
                    share = amounts / count_cap
                    root = jnp.sqrt(share)
                    w = jnp.minimum(1.0, root * jnp.sqrt(root))
                    weight[s, h * HALF:(h + 1) * HALF] = jnp.where(s < live, w, 0.0)
                    target[s, h * HALF:(h + 1) * HALF] = jnp.log(jnp.maximum(amounts, 1.0))
            ids.wait_recv()
            fetch = pltpu.make_async_copy(orow_in, orow, in_sem.at[8])
            fetch.start()
            fetch.wait()

        wait_bytes(rowb.at[step, pl.ds(0, NEAR)], ag_rs.at[step, 0])
        wait_bytes(rowbuf.at[step, pl.ds(0, NEAR)], ag_rs.at[step, 2])
        for s in range(NT):
            xsend[step, s] = rowbuf[step, orow[s]]
            xbsend[step, s] = rowb[step, orow[s]]
        cross = remote(xsend.at[step], xrecv.at[step], x_ss.at[step, 0], x_rs.at[step, 0], other)
        bcross = remote(xbsend.at[step], xbrecv.at[step], x_ss.at[step, 1], x_rs.at[step, 1], other)
        cross.start()
        bcross.start()
        wait_bytes(colb.at[step, pl.ds(0, NEAR)], ag_rs.at[step, 1])
        wait_bytes(colbuf.at[step, pl.ds(0, NEAR)], ag_rs.at[step, 3])
        cross.wait_recv()
        bcross.wait_recv()

        e_is, resids, lefts = [], [], []
        for s in range(NT):
            ti, tj = trow[s], tcol[s]
            e_i = jnp.concatenate([rowbuf[step, ti], xrecv[step, s]], axis=0)
            e_j = colbuf[step, pl.ds(2 * tj, 2)].reshape(TILE, D)
            b_i = jnp.where(low, rowb[step, ti], xbrecv[step, s])
            b_j = jnp.where(low, colb[step, 2 * tj], colb[step, 2 * tj + 1])
            lhs = jnp.where(first_row == 0, b_i, jnp.where(first_row == 1, 1.0, 0.0)).astype(BF16)
            rhs = jnp.where(first_row == 0, 1.0, jnp.where(first_row == 1, b_j, 0.0)).astype(BF16)
            score = dot(e_i, e_j, ((1,), (1,))) + dot(lhs, rhs, ((0,), (0,)))
            resid = (weight[s] * (score - target[s])).astype(BF16)
            e_is.append(e_i)
            resids.append(resid)
            lefts.append((dot(resid, e_j, ((1,), (0,))), dot(one_rows, resid, ((1,), (1,)))[0:1]))

        def merged(terms, ids):
            for s in range(NT):
                total, btotal = terms[s]
                for o in range(NT):
                    if o != s:
                        same = jnp.where(ids[o] == ids[s], 1.0, 0.0)
                        total = total + same * terms[o][0]
                        btotal = btotal + same * terms[o][1]
                yield s, total.astype(BF16), btotal

        for s, total, btotal in merged(lefts, trow):
            gown[s] = total[0:HALF]
            goth[step, s] = total[HALF:TILE]
            gbias[s] = btotal
        hcross = remote(goth.at[step], hrecv.at[pl.ds(0, NT)], x_ss.at[step, 2], x_rs.at[step, 2], other)
        hbcross = remote(gbias.at[pl.ds(0, NT)], hbrecv.at[pl.ds(0, NT)], x_ss.at[step, 3], x_rs.at[step, 3], other)
        hcross.start()
        hbcross.start()

        rights = [
            (dot(resids[s], e_is[s], ((0,), (0,))), dot(one_rows, resids[s], ((1,), (0,)))[0:1]) for s in range(NT)
        ]
        for s, total, btotal in merged(rights, tcol):
            gright[s] = total.reshape(2, HALF, D)
            cbias[s] = btotal

        def slot_of(ids, tile):
            found = jnp.int32(NT)
            for s in range(NT):
                found = jnp.where(ids[s] == tile, s, found)
            return found

        for t in range(COL_TILES):
            slot = slot_of(tcol, t)
            csend[step, 2 * t:2 * t + 2] = gright[slot]
            cbsend[step, 2 * t] = cbias[slot]
            cbsend[step, 2 * t + 1] = cbias[slot]
        for k, off in enumerate(COL_OFF):
            to = col_rank(off)
            remote(cbsend.at[step, to], cbrecv.at[step, k], rsb_ss.at[step, 1], rsb_rs.at[step, 1], (to, c)).start()
        for k, off in enumerate(COL_OFF):
            to = col_rank(off)
            remote(csend.at[step, to], crecv.at[step, k], rs_ss.at[step, 1],
                   rs_rs.at[step, 1, k // PER], (to, c)).start()

        hcross.wait_recv()
        hbcross.wait_recv()
        for t in range(ROW_TILES):
            mine, its = slot_of(trow, t), slot_of(orow, t)
            rsend[step, t] = gown[mine] + hrecv[its]
            rbsend[step, t] = gbias[mine] + pltpu.roll(hbrecv[its], HALF, 1)
        for k, off in enumerate(ROW_OFF):
            to = row_chip(off)
            remote(rbsend.at[step, to], rbrecv.at[step, k], rsb_ss.at[step, 0], rsb_rs.at[step, 0],
                   (r, to * 2 + co)).start()
        for k, off in enumerate(ROW_OFF):
            to = row_chip(off)
            remote(rsend.at[step, to], rrecv.at[step, k], rs_ss.at[step, 0],
                   rs_rs.at[step, 0, k // PER], (r, to * 2 + co)).start()

        g = rsend[step, chip].astype(F32) + csend[step, r].astype(F32)
        wait_bytes(cbrecv.at[step], rsb_rs.at[step, 1])
        wait_bytes(rbrecv.at[step], rsb_rs.at[step, 0])
        row_b, col_b = rbsend[step, chip], cbsend[step, r]
        for k in range(NEAR):
            row_b = row_b + rbrecv[step, k]
            col_b = col_b + cbrecv[step, k]
        for half_id, store in ((1, crecv), (0, rrecv)):
            for group in range(GROUPS):
                wait_bytes(store.at[step, pl.ds(group * PER, PER)], rs_rs.at[step, half_id, group])
                for k in range(group * PER, (group + 1) * PER):
                    g = g + store[step, k].astype(F32)

        new_acc = acc[...] + g * g
        new_vals = vals[...] - learn_rate * g / jnp.sqrt(new_acc)
        lane_half = lax.broadcasted_iota(jnp.int32, (1, D), 1) // HALF
        row_b = jnp.where(low, row_b, 0.0)
        col_b = jnp.where(lane_half == z % 2, col_b, 0.0)
        both = row_b + col_b
        bg = both + pltpu.roll(both, HALF, 1)
        new_bacc = bacc[...] + bg * bg
        new_bvals = bvals[...] - learn_rate * bg / jnp.sqrt(new_bacc)
        if step + 1 < STEPS:
            vals[...] = new_vals
            acc[...] = new_acc
            bvals[...] = new_bvals
            bacc[...] = new_bacc
        else:
            emb_out[...] = new_vals
            bias_out[...] = new_bvals[:, 0:HALF]

        if step == 0:
            ids.wait_send()
        for sem, ref in (
            (ag_ss.at[step, 0], rbrecv), (ag_ss.at[step, 1], rbrecv),
            (ag_ss.at[step, 2], rrecv), (ag_ss.at[step, 3], rrecv),
            (rs_ss.at[step, 0], rrecv), (rs_ss.at[step, 1], rrecv),
            (rsb_ss.at[step, 0], rbrecv), (rsb_ss.at[step, 1], rbrecv),
        ):
            wait_bytes(ref.at[step], sem)
        for copy in (cross, bcross, hcross, hbcross):
            copy.wait_send()


def per_device(emb, bias, emb_sq, bias_sq, tile_rows, tile_cols, tile_live, counts):
    hbm = pl.BlockSpec(memory_space=pltpu.HBM)
    vmem = pl.BlockSpec(memory_space=pltpu.VMEM)
    emb_out, bias_out = pl.pallas_call(
        body,
        out_shape=(jax.ShapeDtypeStruct((HALF, D), F32), jax.ShapeDtypeStruct((1, HALF), F32)),
        in_specs=[hbm] * 8,
        out_specs=(vmem, vmem),
        scratch_shapes=[
            pltpu.VMEM((HALF, D), F32),
            pltpu.VMEM((1, HALF), F32),
            pltpu.VMEM((HALF, D), F32),
            pltpu.VMEM((1, HALF), F32),
            pltpu.VMEM((1, D), F32),
            pltpu.VMEM((1, D), F32),
            pltpu.VMEM((NT, TILE, TILE), jnp.int32),
            pltpu.VMEM((NT, TILE, TILE), F32),
            pltpu.VMEM((NT, TILE, TILE), F32),
            pltpu.SMEM((NT,), jnp.int32),
            pltpu.SMEM((NT,), jnp.int32),
            pltpu.SMEM((1,), jnp.int32),
            pltpu.VMEM((NT,), jnp.int32),
            pltpu.SMEM((NT,), jnp.int32),
            pltpu.VMEM((STEPS, HALF, D), BF16),
            pltpu.VMEM((STEPS, 1, D), F32),
            pltpu.VMEM((STEPS, ROW_TILES, HALF, D), BF16),
            pltpu.VMEM((STEPS, ROW_TILES, 1, D), F32),
            pltpu.VMEM((STEPS, 2 * COL_TILES, HALF, D), BF16),
            pltpu.VMEM((STEPS, 2 * COL_TILES, 1, D), F32),
            pltpu.VMEM((STEPS, NT, HALF, D), BF16),
            pltpu.VMEM((STEPS, NT, 1, D), F32),
            pltpu.VMEM((STEPS, NT, HALF, D), BF16),
            pltpu.VMEM((STEPS, NT, 1, D), F32),
            pltpu.VMEM((NT + 1, HALF, D), BF16),
            pltpu.VMEM((STEPS, NT, HALF, D), BF16),
            pltpu.VMEM((NT + 1, 1, D), F32),
            pltpu.VMEM((NT + 1, 2, HALF, D), BF16),
            pltpu.VMEM((NT + 1, 1, D), F32),
            pltpu.VMEM((NT + 1, HALF, D), BF16),
            pltpu.VMEM((NT + 1, 1, D), F32),
            pltpu.VMEM((STEPS, ROW_TILES, HALF, D), BF16),
            pltpu.VMEM((STEPS, ROW_TILES, 1, D), F32),
            pltpu.VMEM((STEPS, NEAR, HALF, D), BF16),
            pltpu.VMEM((STEPS, NEAR, 1, D), F32),
            pltpu.VMEM((STEPS, 2 * COL_TILES, HALF, D), BF16),
            pltpu.VMEM((STEPS, 2 * COL_TILES, 1, D), F32),
            pltpu.VMEM((STEPS, NEAR, HALF, D), BF16),
            pltpu.VMEM((STEPS, NEAR, 1, D), F32),
            pltpu.SemaphoreType.DMA((9,)),
            pltpu.SemaphoreType.DMA,
            pltpu.SemaphoreType.DMA,
            pltpu.SemaphoreType.DMA((STEPS, 4)),
            pltpu.SemaphoreType.DMA((STEPS, 4)),
            pltpu.SemaphoreType.DMA((STEPS, 4)),
            pltpu.SemaphoreType.DMA((STEPS, 4)),
            pltpu.SemaphoreType.DMA((STEPS, 2)),
            pltpu.SemaphoreType.DMA((STEPS, 2, GROUPS)),
            pltpu.SemaphoreType.DMA((STEPS, 2)),
            pltpu.SemaphoreType.DMA((STEPS, 2)),
        ],
        compiler_params=pltpu.CompilerParams(
            collective_id=0, has_side_effects=True, vmem_limit_bytes=56 * 1024 * 1024
        ),
    )(
        emb, bias.reshape(1, HALF), emb_sq, bias_sq.reshape(1, HALF), counts,
        tile_rows, tile_cols, tile_live,
    )
    return (emb_out, bias_out.reshape(HALF))


def solution(mesh):
    placed = (
        P(("row", "col"), None),
        P(("row", "col")),
        P(("row", "col"), None),
        P(("row", "col")),
        P(("row", "col")),
        P(("row", "col")),
        P(("row", "col")),
        P(("row", "col"), None, None),
    )
    return jax.shard_map(
        per_device,
        mesh=mesh,
        in_specs=placed,
        out_specs=(P(("row", "col"), None), P(("row", "col"))),
        check_vma=False,
    )
```

time: 907 us -> 58.7 us (0.06)
  blocking collectives: 516 us -> 0 us
  waiting for transfers between devices: 350 us -> 0 us
  Pallas kernels: 0 us -> 55.3 us
  between operations: 17.3 us -> 1.3 us
  local copies, waits for them, and re-layouts: 12.1 us -> 1.89 us
    unnamed x8 -> x0, blocking collectives: 354 us -> none
    reduce_scatter x4 -> x0, waiting for transfers between devices: 350 us -> none  [the longest x2 242 us: return_rows(): lax.psum_scatter(row_part.astype(jnp.bfloat16), 'col', scatter_dimension=...]
    all_gather x4 -> x0, blocking collectives: 163 us -> none  [the longest x2 85.4 us: per_device(): lax.all_gather(emb_half, 'col', axis=0, tiled=True)]
    pallas_call x0 -> x1, Pallas kernels: none -> 55.3 us  [per_device(): pl.pallas_call(body, out_shape=(jax.ShapeDtypeStruct((HALF, D), F32), jax...]
  transfers between devices with their start and end apart: 4 -> 0, of which waited for: 4 -> 0; matrix products, arithmetic and copies ran while one was open for 1% -> 0% of each run, Pallas kernels for 0% -> 0%
where the time goes in v2:
time: 58.7 us; the launch traced here: 58.5 us
  Pallas kernels  55.3 us (94%)
  local copies, waits for them, and re-layouts  1.89 us (3%)
  between operations  1.3 us (2%)
    pallas_call x1, Pallas kernels, per_device(): pl.pallas_call(body, out_shape=(jax.ShapeDtypeStruct((HALF, D), F32), jax...  55.3 us
    unnamed x4, local copies, waits for them, and re-layouts  1.89 us

profile of v2, /device:TPU:1, one launch (start us, length us, event | category | flops | bytes accessed | tf_op | source)
XLA Modules:
  0.0 58.5 jit_solution(1387942575256855137)
XLA Ops:
  1.3 55.3 %shard_map.95 = (f32[64,128]{1,0:T(8,128)}, f32[1,64]{1,0:T(1,128)}) custom-call(f32[64,128]{1,0:T(8,128)} %emb_hbm.1, f32[1,64]{1,0:T(1,128)} %bitcast.3, f32[64,128]{1,0:T(8,128)} %esq_hbm.1, f32[1,64]{1,0:T(1,128)} %bitcast.4, s32[4,128,128]{2,1,0:T(8,128)} %counts_hbm.1, s32[4]{0:T(128)} %trow_hbm.1, s32[4]{0:T(128)} %tcol_hbm.1, s32[1]{0:T(128)S(6)} %copy.12.tlive_hbm), custom_call_target="tpu_custom_call" | custom-call | tf_op jit(solution)/shard_map/pallas_call | solution.py:274
  56.6 0.0 copy-start
  56.6 1.4 %copy.13 = f32[64,128]{1,0:T(8,128)} copy(f32[64,128]{1,0:T(8,128)} %get-tuple-element.8) | data formatting | bytes 65536
  58.0 0.0 copy-done
  58.0 0.5 copy.14
Async XLA Ops:
  56.6 1.4 %copy-start = (f32[1,64]{1,0:T(1,128)S(1)}, f32[1,64]{1,0:T(1,128)}, u32[]{:S(2)}) copy-start(f32[1,64]{1,0:T(1,128)} %get-tuple-element.5) | copy-start | bytes 772

commit v3 on v2

--- a/solution.py
+++ b/solution.py
@@ -33,10 +33,10 @@
 
 
 def body(
-    emb_hbm, bias_hbm, esq_hbm, bsq_hbm, counts_hbm, trow_hbm, tcol_hbm, tlive_hbm,
+    emb_hbm, bias_hbm, esq_hbm, bsq_hbm, counts_hbm, trow_hbm, tcol_hbm, tlive,
     emb_out, bias_out,
     vals, bhalf, acc, bsqhalf, bvals, bacc, cnt, weight, target,
-    trow, tcol, tlive, orow_in, orow,
+    trow, tcol, orow_in, orow,
     msg, bmsg, rowbuf, rowb, colbuf, colb, xsend, xbsend, xrecv, xbrecv,
     gown, goth, gbias, gright, cbias, hrecv, hbrecv,
     rsend, rbsend, rrecv, rbrecv, csend, cbsend, crecv, cbrecv,
@@ -68,18 +68,18 @@
         for i, (src, dst) in enumerate(
             (
                 (emb_hbm, vals), (bias_hbm, bhalf), (esq_hbm, acc), (bsq_hbm, bsqhalf),
-                (counts_hbm, cnt), (trow_hbm, trow), (tcol_hbm, tcol), (tlive_hbm, tlive),
+                (counts_hbm, cnt), (trow_hbm, trow), (tcol_hbm, tcol),
             )
         )
     ]
-    for load in loads:
-        load.start()
-
     barrier = pltpu.get_barrier_semaphore()
     for row_off, col_off in zip(ROW_OFF, COL_OFF):
         pl.semaphore_signal(barrier, inc=1, device_id=(col_rank(col_off), c), device_id_type=MESH)
         pl.semaphore_signal(barrier, inc=1, device_id=(r, row_chip(row_off) * 2 + co), device_id_type=MESH)
     pl.semaphore_signal(barrier, inc=1, device_id=other, device_id_type=MESH)
+
+    for load in loads:
+        load.start()
 
     for load in loads[:4] + loads[5:]:
         load.wait()
@@ -104,15 +104,12 @@
         bhalf_now = bvals[...].astype(BF16).astype(F32)
         bmsg[step] = bhalf_now
         for row_off, col_off in zip(ROW_OFF, COL_OFF):
-            remote(bmsg.at[step], rowb.at[step, chip], ag_ss.at[step, 0], ag_rs.at[step, 0],
-                   (r, row_chip(row_off) * 2 + co)).start()
-            remote(bmsg.at[step], colb.at[step, r], ag_ss.at[step, 1], ag_rs.at[step, 1],
-                   (col_rank(col_off), c)).start()
-        for row_off, col_off in zip(ROW_OFF, COL_OFF):
-            remote(msg.at[step], rowbuf.at[step, chip], ag_ss.at[step, 2], ag_rs.at[step, 2],
-                   (r, row_chip(row_off) * 2 + co)).start()
-            remote(msg.at[step], colbuf.at[step, r], ag_ss.at[step, 3], ag_rs.at[step, 3],
-                   (col_rank(col_off), c)).start()
+            to = (col_rank(col_off), c)
+            remote(msg.at[step], colbuf.at[step, r], ag_ss.at[step, 3], ag_rs.at[step, 3], to).start()
+            remote(bmsg.at[step], colb.at[step, r], ag_ss.at[step, 1], ag_rs.at[step, 1], to).start()
+            to = (r, row_chip(row_off) * 2 + co)
+            remote(msg.at[step], rowbuf.at[step, chip], ag_ss.at[step, 2], ag_rs.at[step, 2], to).start()
+            remote(bmsg.at[step], rowb.at[step, chip], ag_ss.at[step, 0], ag_rs.at[step, 0], to).start()
         rowbuf[step, chip] = half
         colbuf[step, r] = half
         rowb[step, chip] = bhalf_now
@@ -131,7 +128,7 @@
                     weight[s, h * HALF:(h + 1) * HALF] = jnp.where(s < live, w, 0.0)
                     target[s, h * HALF:(h + 1) * HALF] = jnp.log(jnp.maximum(amounts, 1.0))
             ids.wait_recv()
-            fetch = pltpu.make_async_copy(orow_in, orow, in_sem.at[8])
+            fetch = pltpu.make_async_copy(orow_in, orow, in_sem.at[7])
             fetch.start()
             fetch.wait()
 
@@ -203,11 +200,9 @@
             cbsend[step, 2 * t + 1] = cbias[slot]
         for k, off in enumerate(COL_OFF):
             to = col_rank(off)
-            remote(cbsend.at[step, to], cbrecv.at[step, k], rsb_ss.at[step, 1], rsb_rs.at[step, 1], (to, c)).start()
-        for k, off in enumerate(COL_OFF):
-            to = col_rank(off)
             remote(csend.at[step, to], crecv.at[step, k], rs_ss.at[step, 1],
                    rs_rs.at[step, 1, k // PER], (to, c)).start()
+            remote(cbsend.at[step, to], cbrecv.at[step, k], rsb_ss.at[step, 1], rsb_rs.at[step, 1], (to, c)).start()
 
         hcross.wait_recv()
         hbcross.wait_recv()
@@ -217,25 +212,24 @@
             rbsend[step, t] = gbias[mine] + pltpu.roll(hbrecv[its], HALF, 1)
         for k, off in enumerate(ROW_OFF):
             to = row_chip(off)
-            remote(rbsend.at[step, to], rbrecv.at[step, k], rsb_ss.at[step, 0], rsb_rs.at[step, 0],
-                   (r, to * 2 + co)).start()
-        for k, off in enumerate(ROW_OFF):
-            to = row_chip(off)
+            device = (r, to * 2 + co)
             remote(rsend.at[step, to], rrecv.at[step, k], rs_ss.at[step, 0],
-                   rs_rs.at[step, 0, k // PER], (r, to * 2 + co)).start()
+                   rs_rs.at[step, 0, k // PER], device).start()
+            remote(rbsend.at[step, to], rbrecv.at[step, k], rsb_ss.at[step, 0], rsb_rs.at[step, 0], device).start()
 
         g = rsend[step, chip].astype(F32) + csend[step, r].astype(F32)
+        for half_id, store in ((1, crecv), (0, rrecv)):
+            for group in range(GROUPS):
+                wait_bytes(store.at[step, pl.ds(group * PER, PER)], rs_rs.at[step, half_id, group])
+                for k in range(group * PER, (group + 1) * PER):
+                    g = g + store[step, k].astype(F32)
+
         wait_bytes(cbrecv.at[step], rsb_rs.at[step, 1])
         wait_bytes(rbrecv.at[step], rsb_rs.at[step, 0])
         row_b, col_b = rbsend[step, chip], cbsend[step, r]
         for k in range(NEAR):
             row_b = row_b + rbrecv[step, k]
             col_b = col_b + cbrecv[step, k]
-        for half_id, store in ((1, crecv), (0, rrecv)):
-            for group in range(GROUPS):
-                wait_bytes(store.at[step, pl.ds(group * PER, PER)], rs_rs.at[step, half_id, group])
-                for k in range(group * PER, (group + 1) * PER):
-                    g = g + store[step, k].astype(F32)
 
         new_acc = acc[...] + g * g
         new_vals = vals[...] - learn_rate * g / jnp.sqrt(new_acc)
@@ -274,7 +268,7 @@
     emb_out, bias_out = pl.pallas_call(
         body,
         out_shape=(jax.ShapeDtypeStruct((HALF, D), F32), jax.ShapeDtypeStruct((1, HALF), F32)),
-        in_specs=[hbm] * 8,
+        in_specs=[hbm] * 7 + [pl.BlockSpec(memory_space=pltpu.SMEM)],
         out_specs=(vmem, vmem),
         scratch_shapes=[
             pltpu.VMEM((HALF, D), F32),
@@ -288,7 +282,6 @@
             pltpu.VMEM((NT, TILE, TILE), F32),
             pltpu.SMEM((NT,), jnp.int32),
             pltpu.SMEM((NT,), jnp.int32),
-            pltpu.SMEM((1,), jnp.int32),
             pltpu.VMEM((NT,), jnp.int32),
             pltpu.SMEM((NT,), jnp.int32),
             pltpu.VMEM((STEPS, HALF, D), BF16),
@@ -316,7 +309,7 @@
             pltpu.VMEM((STEPS, 2 * COL_TILES, 1, D), F32),
             pltpu.VMEM((STEPS, NEAR, HALF, D), BF16),
             pltpu.VMEM((STEPS, NEAR, 1, D), F32),
-            pltpu.SemaphoreType.DMA((9,)),
+            pltpu.SemaphoreType.DMA((8,)),
             pltpu.SemaphoreType.DMA,
             pltpu.SemaphoreType.DMA,
             pltpu.SemaphoreType.DMA((STEPS, 4)),
@@ -329,11 +322,17 @@
             pltpu.SemaphoreType.DMA((STEPS, 2)),
         ],
         compiler_params=pltpu.CompilerParams(
-            collective_id=0, has_side_effects=True, vmem_limit_bytes=56 * 1024 * 1024
+            collective_id=0, has_side_effects=True, vmem_limit_bytes=40 * 1024 * 1024
         ),
     )(
-        emb, bias.reshape(1, HALF), emb_sq, bias_sq.reshape(1, HALF), counts,
-        tile_rows, tile_cols, tile_live,
+        *(
+            pltpu.with_memory_space_constraint(v, pltpu.HBM)
+            for v in (
+                emb, bias.reshape(1, HALF), emb_sq, bias_sq.reshape(1, HALF), counts,
+                tile_rows, tile_cols,
+            )
+        ),
+        tile_live,
     )
     return (emb_out, bias_out.reshape(HALF))
 

time: 58.7 us -> 57.3 us (0.976)
  local copies, waits for them, and re-layouts: 1.89 us -> 1.13 us
  Pallas kernels: 55.3 us -> 54.7 us
    unnamed x4 -> x2, local copies, waits for them, and re-layouts: 1.89 us -> 1.13 us
    pallas_call x1, Pallas kernels: 55.3 us -> 54.7 us  [per_device(): pl.pallas_call(body, out_shape=(jax.ShapeDtypeStruct((HALF, D), F32), jax...]
where the time goes in v3:
time: 57.3 us; the launch traced here: 57.1 us
  Pallas kernels  54.7 us (95%)
  between operations  1.29 us (2%)
  local copies, waits for them, and re-layouts  1.13 us (2%)
    pallas_call x1, Pallas kernels, per_device(): pl.pallas_call(body, out_shape=(jax.ShapeDtypeStruct((HALF, D), F32), jax...  54.7 us

profile of v3, /device:TPU:1, one launch (start us, length us, event | category | flops | bytes accessed | tf_op | source)
XLA Modules:
  0.0 57.1 jit_solution(14213047325170365104)
XLA Ops:
  1.3 54.7 %shard_map.95 = (f32[64,128]{1,0:T(8,128)S(1)}, f32[1,64]{1,0:T(1,128)S(1)}) custom-call(f32[64,128]{1,0:T(8,128)} %emb_hbm.1, f32[1,64]{1,0:T(1,128)} %bitcast.4, f32[64,128]{1,0:T(8,128)} %esq_hbm.1, f32[1,64]{1,0:T(1,128)} %bitcast.5, s32[4,128,128]{2,1,0:T(8,128)} %counts_hbm.1, s32[4]{0:T(128)} %trow_hbm.1, s32[4]{0:T(128)} %tcol_hbm.1, s32[1]{0:T(128)S(6)} %copy.12.tlive), custom_call_target="tpu_custom_call" | custom-call | tf_op jit(solution)/shard_map/pallas_call | solution.py:268
  56.0 0.6 %copy.13 = f32[64,128]{1,0:T(8,128)} copy(f32[64,128]{1,0:T(8,128)S(1)} %get-tuple-element.8) | data formatting | bytes 65536
  56.6 0.5 copy.14

commit v4 on v3

--- a/solution.py
+++ b/solution.py
@@ -16,6 +16,10 @@
 NEAR = 15
 GROUPS = 3
 PER = NEAR // GROUPS
+WHOLE = [(0, HALF)]
+SPLIT = [(0, HALF // 2), (HALF // 2, HALF // 2)]
+GATHER_PARTS = [WHOLE] + [SPLIT] * (STEPS - 1)
+RETURN_PARTS = [SPLIT] * (STEPS - 1) + [WHOLE]
 
 learn_rate = 0.1
 count_cap = 100.0
@@ -34,7 +38,7 @@
 
 def body(
     emb_hbm, bias_hbm, esq_hbm, bsq_hbm, counts_hbm, trow_hbm, tcol_hbm, tlive,
-    emb_out, bias_out,
+    out,
     vals, bhalf, acc, bsqhalf, bvals, bacc, cnt, weight, target,
     trow, tcol, orow_in, orow,
     msg, bmsg, rowbuf, rowb, colbuf, colb, xsend, xbsend, xrecv, xbrecv,
@@ -98,23 +102,31 @@
     pl.semaphore_wait(barrier, 2 * NEAR + 1)
 
     ids = remote(trow_hbm, orow_in, id_ss, id_rs, other)
-    for step in range(STEPS):
-        half = vals[...].astype(BF16)
-        msg[step] = half
-        bhalf_now = bvals[...].astype(BF16).astype(F32)
-        bmsg[step] = bhalf_now
+    def send_gather(step, part, with_bias):
+        lo, n = GATHER_PARTS[step][part]
+        rows = pl.ds(lo, n)
+        half = vals[lo:lo + n].astype(BF16)
+        msg[step, lo:lo + n] = half
+        if with_bias:
+            bhalf_now = bvals[...].astype(BF16).astype(F32)
+            bmsg[step] = bhalf_now
         for row_off, col_off in zip(ROW_OFF, COL_OFF):
             to = (col_rank(col_off), c)
-            remote(msg.at[step], colbuf.at[step, r], ag_ss.at[step, 3], ag_rs.at[step, 3], to).start()
-            remote(bmsg.at[step], colb.at[step, r], ag_ss.at[step, 1], ag_rs.at[step, 1], to).start()
+            remote(msg.at[step, rows], colbuf.at[step, r, rows], ag_ss.at[step, 3], ag_rs.at[step, 3, part], to).start()
+            if with_bias:
+                remote(bmsg.at[step], colb.at[step, r], ag_ss.at[step, 1], ag_rs.at[step, 1, 0], to).start()
             to = (r, row_chip(row_off) * 2 + co)
-            remote(msg.at[step], rowbuf.at[step, chip], ag_ss.at[step, 2], ag_rs.at[step, 2], to).start()
-            remote(bmsg.at[step], rowb.at[step, chip], ag_ss.at[step, 0], ag_rs.at[step, 0], to).start()
-        rowbuf[step, chip] = half
-        colbuf[step, r] = half
-        rowb[step, chip] = bhalf_now
-        colb[step, r] = bhalf_now
-
+            remote(msg.at[step, rows], rowbuf.at[step, chip, rows], ag_ss.at[step, 2], ag_rs.at[step, 2, part], to).start()
+            if with_bias:
+                remote(bmsg.at[step], rowb.at[step, chip], ag_ss.at[step, 0], ag_rs.at[step, 0, 0], to).start()
+        rowbuf[step, chip, lo:lo + n] = half
+        colbuf[step, r, lo:lo + n] = half
+        if with_bias:
+            rowb[step, chip] = bhalf_now
+            colb[step, r] = bhalf_now
+
+    send_gather(0, 0, True)
+    for step in range(STEPS):
         if step == 0:
             ids.start()
             loads[4].wait()
@@ -132,8 +144,9 @@
             fetch.start()
             fetch.wait()
 
-        wait_bytes(rowb.at[step, pl.ds(0, NEAR)], ag_rs.at[step, 0])
-        wait_bytes(rowbuf.at[step, pl.ds(0, NEAR)], ag_rs.at[step, 2])
+        for part, (lo, n) in enumerate(GATHER_PARTS[step]):
+            wait_bytes(rowbuf.at[step, pl.ds(0, NEAR), pl.ds(lo, n)], ag_rs.at[step, 2, part])
+        wait_bytes(rowb.at[step, pl.ds(0, NEAR)], ag_rs.at[step, 0, 0])
         for s in range(NT):
             xsend[step, s] = rowbuf[step, orow[s]]
             xbsend[step, s] = rowb[step, orow[s]]
@@ -141,8 +154,9 @@
         bcross = remote(xbsend.at[step], xbrecv.at[step], x_ss.at[step, 1], x_rs.at[step, 1], other)
         cross.start()
         bcross.start()
-        wait_bytes(colb.at[step, pl.ds(0, NEAR)], ag_rs.at[step, 1])
-        wait_bytes(colbuf.at[step, pl.ds(0, NEAR)], ag_rs.at[step, 3])
+        for part, (lo, n) in enumerate(GATHER_PARTS[step]):
+            wait_bytes(colbuf.at[step, pl.ds(0, NEAR), pl.ds(lo, n)], ag_rs.at[step, 3, part])
+        wait_bytes(colb.at[step, pl.ds(0, NEAR)], ag_rs.at[step, 1, 0])
         cross.wait_recv()
         bcross.wait_recv()
 
@@ -198,11 +212,32 @@
             csend[step, 2 * t:2 * t + 2] = gright[slot]
             cbsend[step, 2 * t] = cbias[slot]
             cbsend[step, 2 * t + 1] = cbias[slot]
-        for k, off in enumerate(COL_OFF):
-            to = col_rank(off)
-            remote(csend.at[step, to], crecv.at[step, k], rs_ss.at[step, 1],
-                   rs_rs.at[step, 1, k // PER], (to, c)).start()
-            remote(cbsend.at[step, to], cbrecv.at[step, k], rsb_ss.at[step, 1], rsb_rs.at[step, 1], (to, c)).start()
+        parts = RETURN_PARTS[step]
+
+        def send_columns(part):
+            lo, n = parts[part]
+            for k, off in enumerate(COL_OFF):
+                to = col_rank(off)
+                sem = rs_rs.at[step, 1, part if len(parts) > 1 else k // PER]
+                remote(csend.at[step, to, pl.ds(lo, n)], crecv.at[step, k, pl.ds(lo, n)],
+                       rs_ss.at[step, 1], sem, (to, c)).start()
+                if part == 0:
+                    remote(cbsend.at[step, to], cbrecv.at[step, k],
+                           rsb_ss.at[step, 1], rsb_rs.at[step, 1], (to, c)).start()
+
+        def send_rows(part):
+            lo, n = parts[part]
+            for k, off in enumerate(ROW_OFF):
+                to = row_chip(off)
+                device = (r, to * 2 + co)
+                sem = rs_rs.at[step, 0, part if len(parts) > 1 else k // PER]
+                remote(rsend.at[step, to, pl.ds(lo, n)], rrecv.at[step, k, pl.ds(lo, n)],
+                       rs_ss.at[step, 0], sem, device).start()
+                if part == 0:
+                    remote(rbsend.at[step, to], rbrecv.at[step, k],
+                           rsb_ss.at[step, 0], rsb_rs.at[step, 0], device).start()
+
+        send_columns(0)
 
         hcross.wait_recv()
         hbcross.wait_recv()
@@ -210,44 +245,50 @@
             mine, its = slot_of(trow, t), slot_of(orow, t)
             rsend[step, t] = gown[mine] + hrecv[its]
             rbsend[step, t] = gbias[mine] + pltpu.roll(hbrecv[its], HALF, 1)
-        for k, off in enumerate(ROW_OFF):
-            to = row_chip(off)
-            device = (r, to * 2 + co)
-            remote(rsend.at[step, to], rrecv.at[step, k], rs_ss.at[step, 0],
-                   rs_rs.at[step, 0, k // PER], device).start()
-            remote(rbsend.at[step, to], rbrecv.at[step, k], rsb_ss.at[step, 0], rsb_rs.at[step, 0], device).start()
-
-        g = rsend[step, chip].astype(F32) + csend[step, r].astype(F32)
-        for half_id, store in ((1, crecv), (0, rrecv)):
-            for group in range(GROUPS):
-                wait_bytes(store.at[step, pl.ds(group * PER, PER)], rs_rs.at[step, half_id, group])
-                for k in range(group * PER, (group + 1) * PER):
-                    g = g + store[step, k].astype(F32)
-
-        wait_bytes(cbrecv.at[step], rsb_rs.at[step, 1])
-        wait_bytes(rbrecv.at[step], rsb_rs.at[step, 0])
-        row_b, col_b = rbsend[step, chip], cbsend[step, r]
-        for k in range(NEAR):
-            row_b = row_b + rbrecv[step, k]
-            col_b = col_b + cbrecv[step, k]
-
-        new_acc = acc[...] + g * g
-        new_vals = vals[...] - learn_rate * g / jnp.sqrt(new_acc)
-        lane_half = lax.broadcasted_iota(jnp.int32, (1, D), 1) // HALF
-        row_b = jnp.where(low, row_b, 0.0)
-        col_b = jnp.where(lane_half == z % 2, col_b, 0.0)
-        both = row_b + col_b
-        bg = both + pltpu.roll(both, HALF, 1)
-        new_bacc = bacc[...] + bg * bg
-        new_bvals = bvals[...] - learn_rate * bg / jnp.sqrt(new_bacc)
-        if step + 1 < STEPS:
-            vals[...] = new_vals
-            acc[...] = new_acc
-            bvals[...] = new_bvals
-            bacc[...] = new_bacc
-        else:
-            emb_out[...] = new_vals
-            bias_out[...] = new_bvals[:, 0:HALF]
+        send_rows(0)
+        for part in range(1, len(parts)):
+            send_columns(part)
+            send_rows(part)
+
+        last = step + 1 == STEPS
+        for part, (lo, n) in enumerate(parts):
+            g = rsend[step, chip, lo:lo + n].astype(F32) + csend[step, r, lo:lo + n].astype(F32)
+            for side, store in ((1, crecv), (0, rrecv)):
+                if len(parts) > 1:
+                    wait_bytes(store.at[step, pl.ds(0, NEAR), pl.ds(lo, n)], rs_rs.at[step, side, part])
+                for k in range(NEAR):
+                    if len(parts) == 1 and k % PER == 0:
+                        wait_bytes(store.at[step, pl.ds(k, PER)], rs_rs.at[step, side, k // PER])
+                    g = g + store[step, k, lo:lo + n].astype(F32)
+            new_acc = acc[lo:lo + n] + g * g
+            new_vals = vals[lo:lo + n] - learn_rate * g / jnp.sqrt(new_acc)
+            if last:
+                out[lo:lo + n] = new_vals
+            else:
+                vals[lo:lo + n] = new_vals
+                acc[lo:lo + n] = new_acc
+            if part + 1 < len(parts):
+                if not last:
+                    send_gather(step + 1, part, False)
+                continue
+
+            wait_bytes(cbrecv.at[step], rsb_rs.at[step, 1])
+            wait_bytes(rbrecv.at[step], rsb_rs.at[step, 0])
+            row_b, col_b = rbsend[step, chip], cbsend[step, r]
+            for k in range(NEAR):
+                row_b = row_b + rbrecv[step, k]
+                col_b = col_b + cbrecv[step, k]
+            lane_half = lax.broadcasted_iota(jnp.int32, (1, D), 1) // HALF
+            both = jnp.where(low, row_b, 0.0) + jnp.where(lane_half == z % 2, col_b, 0.0)
+            bg = both + pltpu.roll(both, HALF, 1)
+            new_bacc = bacc[...] + bg * bg
+            new_bvals = bvals[...] - learn_rate * bg / jnp.sqrt(new_bacc)
+            if last:
+                out[HALF:HALF + 8] = jnp.broadcast_to(new_bvals, (8, D))
+            else:
+                bvals[...] = new_bvals
+                bacc[...] = new_bacc
+                send_gather(step + 1, part, True)
 
         if step == 0:
             ids.wait_send()
@@ -265,11 +306,11 @@
 def per_device(emb, bias, emb_sq, bias_sq, tile_rows, tile_cols, tile_live, counts):
     hbm = pl.BlockSpec(memory_space=pltpu.HBM)
     vmem = pl.BlockSpec(memory_space=pltpu.VMEM)
-    emb_out, bias_out = pl.pallas_call(
+    out = pl.pallas_call(
         body,
-        out_shape=(jax.ShapeDtypeStruct((HALF, D), F32), jax.ShapeDtypeStruct((1, HALF), F32)),
+        out_shape=jax.ShapeDtypeStruct((HALF + 8, D), F32),
         in_specs=[hbm] * 7 + [pl.BlockSpec(memory_space=pltpu.SMEM)],
-        out_specs=(vmem, vmem),
+        out_specs=vmem,
         scratch_shapes=[
             pltpu.VMEM((HALF, D), F32),
             pltpu.VMEM((1, HALF), F32),
@@ -313,7 +354,7 @@
             pltpu.SemaphoreType.DMA,
             pltpu.SemaphoreType.DMA,
             pltpu.SemaphoreType.DMA((STEPS, 4)),
-            pltpu.SemaphoreType.DMA((STEPS, 4)),
+            pltpu.SemaphoreType.DMA((STEPS, 4, 2)),
             pltpu.SemaphoreType.DMA((STEPS, 4)),
             pltpu.SemaphoreType.DMA((STEPS, 4)),
             pltpu.SemaphoreType.DMA((STEPS, 2)),
@@ -334,7 +375,7 @@
         ),
         tile_live,
     )
-    return (emb_out, bias_out.reshape(HALF))
+    return (out[:HALF], out[HALF, :HALF])
 
 
 def solution(mesh):

time: 57.3 us -> 55.1 us (0.962)
  Pallas kernels: 54.7 us -> 52.6 us
    pallas_call x1, Pallas kernels: 54.7 us -> 52.6 us  [per_device(): pl.pallas_call(body, out_shape=jax.ShapeDtypeStruct((HALF + 8, D), F32),...]
    unnamed x2 -> x0, local copies, waits for them, and re-layouts: 1.13 us -> none
    slice x0 -> x1, local copies, waits for them, and re-layouts: none -> 0.62 us  [per_device(): return (out[:HALF], out[HALF, :HALF])]
where the time goes in v4:
time: 55.1 us; the launch traced here: 55 us
  Pallas kernels  52.6 us (95%)
  between operations  1.29 us (2%)
  local copies, waits for them, and re-layouts  1.13 us (2%)
    pallas_call x1, Pallas kernels, per_device(): pl.pallas_call(body, out_shape=jax.ShapeDtypeStruct((HALF + 8, D), F32),...  52.6 us

profile of v4, /device:TPU:1, one launch (start us, length us, event | category | flops | bytes accessed | tf_op | source)
XLA Modules:
  0.0 55.0 jit_solution(13923681445915569028)
XLA Ops:
  1.3 52.6 %shard_map.95 = f32[72,128]{1,0:T(8,128)S(1)} custom-call(f32[64,128]{1,0:T(8,128)} %emb_hbm.1, f32[1,64]{1,0:T(1,128)} %bitcast.4, f32[64,128]{1,0:T(8,128)} %esq_hbm.1, f32[1,64]{1,0:T(1,128)} %bitcast.5, s32[4,128,128]{2,1,0:T(8,128)} %counts_hbm.1, s32[4]{0:T(128)} %trow_hbm.1, s32[4]{0:T(128)} %tcol_hbm.1, s32[1]{0:T(128)S(6)} %copy.10.tlive), custom_call_target="tpu_custom_call" | custom-call | tf_op jit(solution)/shard_map/pallas_call | solution.py:309
  53.9 0.5 slice_bitcast_fusion
  54.4 0.6 %slice.6 = f32[64,128]{1,0:T(8,128)} slice(f32[72,128]{1,0:T(8,128)S(1)} %shard_map.95), slice={[0:64], [0:128]} | slice | bytes 65536 | tf_op jit(solution)/shard_map/slice | solution.py:378
